TPU v7x, 128 devices: a whole 4x4x4 slice. The times are simulated.
128 devices in a mesh: draw: 8 (over z_lo, y), width: 8 (over x, core), cores: 2 (over z_hi).
Axes of the slice: x: 4, y: 4, z: 4 (z_hi: 2, z_lo: 2; z = z_hi * 2 + z_lo), core: 2. Of those that a mesh axis runs over, the one named last changes fastest.
Arguments:
- warmth_history: float32 [10, 4096, 2048], P(None, ('draw', 'width', 'cores')), may hold values from 0.9 to 1.1
- fictitious_warmth: float32 [4096, 2048], P('draw', ('width', 'cores')), may hold values from 0.9 to 1.1
- vertex_velocity: float32 [2, 4096, 2048], P(None, 'draw', ('width', 'cores')), may hold values from -6 to 6
- branch_load_tensors: float32 [12, 3, 4096, 2048], P(None, None, 'draw', ('width', 'cores')), may hold values from -2 to 2
- mechanism_lifetimes: float32 [12], replicated, may hold values from 0.3 to 30
- branch_stiffness: float32 [12], replicated, may hold values from 0.005 to 0.025
Outputs:
- fictive_final: float32 [4096, 2048], P('draw', ('width', 'cores'))
- velocity_final: float32 [2, 4096, 2048], P(None, 'draw', ('width', 'cores'))
- modes_final: float32 [12, 3, 4096, 2048], P(None, None, 'draw', ('width', 'cores'))
All inputs are finite; a program needn't handle non-finite values.
Results may differ from a plain program's by a relative error of at most 0.0001.
Values sent between devices are 32-bit elements; how exact they have to be, the bound alone decides.
No kernel may reach another device: no remote copies, remote signals or barrier semaphores. Data moves between devices by JAX's collectives and lax.ppermute only.
A program may use at most 128 MiB of HBM per device.

v0:
```python
import jax
import jax.numpy as jnp
from jax import lax
from jax.sharding import PartitionSpec as P

clock_increment = 1.0
arrhenius_energy = 20.0
coupling_exponent = 0.5
reduced_clock = 3.0


def shifted(shard, axis, by):
    peers = lax.axis_size(axis)
    pairs = [(i, i + by) for i in range(peers) if 0 <= i + by < peers]
    return lax.ppermute(shard, axis, pairs)


def heat_terms(heat_block):
    return (heat_block, arrhenius_energy * coupling_exponent / heat_block - arrhenius_energy)


def strain_field(motion):
    next_row = shifted(motion[:, :1, :], "draw", -1)
    below = jnp.concatenate([motion[:, 1:, :], next_row], axis=1)
    right_here, right_below = shifted((motion[:, :, 0], below[:, :, 0]), ("width", "cores"), -1)
    beside = jnp.concatenate([motion[:, :, 1:], right_here[:, :, None]], axis=2)
    corner = jnp.concatenate([below[:, :, 1:], right_below[:, :, None]], axis=2)
    grad_len = 0.5 * (below + corner - (motion + beside))
    grad_wid = 0.5 * (beside + corner - (motion + below))
    return jnp.stack([grad_len[0], grad_wid[1], 0.5 * (grad_wid[0] + grad_len[1])])


def nodal_field(stress):
    along_len = -0.5 * jnp.stack([stress[0], stress[2]])
    along_wid = -0.5 * jnp.stack([stress[2], stress[1]])
    node_base = -along_len - along_wid
    node_down = along_len - along_wid
    node_right = along_wid - along_len
    node_diag = along_len + along_wid
    left_base, left_diag = shifted(
        (node_right[:, :, -1], node_diag[:, :, -1]), ("width", "cores"), 1
    )
    row_here = node_base + jnp.concatenate([left_base[:, :, None], node_right[:, :, :-1]], axis=2)
    row_next = node_down + jnp.concatenate([left_diag[:, :, None], node_diag[:, :, :-1]], axis=2)
    from_above = shifted(row_next[:, -1:, :], "draw", 1)
    return row_here + jnp.concatenate([from_above, row_next[:, :-1, :]], axis=1)


def relax_mode(stress_mode, relax_time, modulus, strain, multiplier):
    rate_ratio = clock_increment / (relax_time * multiplier)
    kept = jnp.exp(-rate_ratio)
    weight = -jnp.expm1(-rate_ratio) / rate_ratio
    return kept * stress_mode + 2.0 * clock_increment * modulus * weight * strain


def shards(
    warmth_history,
    fictitious_warmth,
    vertex_velocity,
    branch_load_tensors,
    mechanism_lifetimes,
    branch_stiffness,
):
    tick_ordinal = warmth_history.shape[0]
    piece_lines = warmth_history.shape[1]
    entire_breadth = warmth_history.shape[2]
    row_count = vertex_velocity.shape[1]
    col_count = vertex_velocity.shape[2]
    sheet_pieces = warmth_history.reshape(tick_ordinal, 1, piece_lines, entire_breadth)
    arrived_block = lax.all_to_all(
        sheet_pieces, ("width", "cores"), split_axis=3, concat_axis=1, tiled=True
    )
    heat_all, term_all = heat_terms(
        arrived_block.reshape(arrived_block.shape[0], row_count, col_count)
    )
    update_modes = jax.vmap(relax_mode, in_axes=(0, 0, 0, None, None))

    def march_forward(locator_now, state_now):
        fictive_now, motion, mode_state = state_now
        warmth_now = lax.dynamic_index_in_dim(heat_all, locator_now, 0, keepdims=False)
        warming_contribution = lax.dynamic_index_in_dim(term_all, locator_now, 0, keepdims=False)
        multiplier = jnp.exp(
            warming_contribution + arrhenius_energy * (1.0 - coupling_exponent) / fictive_now
        )
        fictive_next = warmth_now + (fictive_now - warmth_now) * jnp.exp(
            -clock_increment / (reduced_clock * multiplier)
        )
        strain = strain_field(motion)
        mode_next = update_modes(
            mode_state, mechanism_lifetimes, branch_stiffness, strain, multiplier
        )
        stress = jnp.sum(mode_next, axis=0)
        motion_next = motion + clock_increment * nodal_field(stress)
        return (fictive_next, motion_next, mode_next)

    return lax.fori_loop(
        0, tick_ordinal, march_forward, (fictitious_warmth, vertex_velocity, branch_load_tensors)
    )


def solution(mesh):
    in_specs = (
        P(None, ("draw", "width", "cores"), None),
        P("draw", ("width", "cores")),
        P(None, "draw", ("width", "cores")),
        P(None, None, "draw", ("width", "cores")),
        P(),
        P(),
    )
    out_specs = (
        P("draw", ("width", "cores")),
        P(None, "draw", ("width", "cores")),
        P(None, None, "draw", ("width", "cores")),
    )
    return jax.shard_map(shards, mesh=mesh, in_specs=in_specs, out_specs=out_specs, check_vma=False)
```

profile of v0, /device:TPU:97, one launch (start us, length us, event | category | flops | bytes accessed | tf_op | source)
XLA Modules:
  0.0 765.7 jit_solution(2050167849661055217)
XLA Ops:
  0.7 8.6 %copy.74 = f32[12,3,512,128]{3,2,1,0:T(8,128)} copy(f32[12,3,512,128]{3,2,1,0:T(8,128)} %param.11) | data formatting | bytes 18874368
  9.9 15.1 %copy.45 = f32[10,1,32,2048]{2,1,0,3:T(1,128)} copy(f32[10,1,32,2048]{3,2,0,1:T(8,128)S(1)} %bitcast.49) | data formatting | bytes 5242880 | tf_op jit(solution)/shard_map/reshape | solution.py:69
  25.6 94.9 %reduce.8 = f32[2048,10,32]{2,1,0:T(8,128)} reduce(f32[2048,10,1,32]{3,2,1,0:T(1,128)} %bitcast.46, f32[]{:T(128)} %broadcast.140), dimensions={2}, to_apply=%bitcast.22.reduce_sub_computation | reduce | bytes 5242884
  120.5 15.1 %reshape.35 = f32[16,1,40960]{2,1,0:T(1,128)} reshape(f32[2048,10,32]{2,1,0:T(8,128)} %reduce.8) | data formatting | bytes 5242880
  135.6 7.6 all-to-all-start
  143.2 39.1 %all-to-all-done = f32[16,1,40960]{2,1,0:T(1,128)S(1)} async-done(((f32[16,1,40960]{2,1,0:T(1,128)}), f32[16,1,40960]{2,1,0:T(1,128)S(1)}, u32[]{:S(2)}, u32[]{:S(2)}) %all-to-all-start) | async-done | bytes 2621472 | tf_op jit(solution)/shard_map/all_to_all | solution.py:70
  182.3 9.2 %reduce.9 = f32[16,40960]{1,0:T(8,128)} reduce(f32[16,1,40960]{2,1,0:T(1,128)S(1)} %all-to-all-done, f32[]{:T(128)} %broadcast.140), dimensions={1}, to_apply=%all_to_all.11.reduce_sub_computation | reduce | bytes 5242884 | tf_op jit(solution)/shard_map/all_to_all | solution.py:70
  191.5 24.0 %reshape.36 = f32[2048,10,1,32]{3,2,1,0:T(1,128)} reshape(f32[16,40960]{1,0:T(8,128)} %reduce.9) | data formatting | bytes 5242880
  215.5 22.0 %copy.46 = f32[10,1,32,2048]{3,1,2,0:T(1,128)S(1)} copy(f32[10,1,32,2048]{2,1,0,3:T(1,128)} %bitcast.47) | data formatting | bytes 5242880 | tf_op jit(solution)/shard_map/all_to_all | solution.py:70
  239.9 3.7 divide_add_fusion
  243.6 521.3 %while.17 = (s32[]{:T(128)}, f32[512,128]{1,0:T(8,128)}, f32[2,512,128]{2,1,0:T(8,128)S(1)}, f32[12,3,512,128]{3,2,1,0:T(8,128)}, f32[10,512,128]{2,1,0:T(8,128)...) while((s32[]{:T(128)}, f32[512,128]{1,0:T(8,128)}, ...), condition=%wide.region_2.3_spmd, body=%wide.region_0.2_spmd.sunk | while | flops 19660812 | bytes 53078544 | solution.py:96
  243.8 4.5 collective-permute-start
  248.5 5.0 collective-permute-start.1
  255.5 4.2 fusion.29
  262.5 5.0 collective-permute-done.2
  268.2 11.8 %fusion.30 = (f32[3,512,128]{2,1,0:T(8,128)S(1)}, f32[12,3,512,128]{3,2,1,0:T(8,128)}) fusion(f32[3,512,128]{2,1,0:T(8,128)S(1)} %pad_maximum_fusion.5, f32[12,512,128]{2,1,0:T(8,128)} %get-tuple-element.262, f32[12,3,512,128]{3,2,1,0:T(8,128)} %get-tuple-element.283, f32[12,512,128]{2,1,0:T(8,128)} %get-tuple-element.263), kind=kLoop, calls=%fused_computation.37.clone.1 | loop fusion | flops 9240576 | bytes 26738688 | tf_op jit(solution)/shard_map/while/body/eval_jaxpr/reduce_sum | solution.py:92
  287.2 4.1 collective-permute-start.4
  293.5 4.3 collective-permute-done.5
  305.0 4.2 fusion.29
  313.2 3.8 collective-permute-done.2
  317.7 11.8 %fusion.30 = (f32[3,512,128]{2,1,0:T(8,128)S(1)}, f32[12,3,512,128]{3,2,1,0:T(8,128)}) fusion(f32[3,512,128]{2,1,0:T(8,128)S(1)} %pad_maximum_fusion.5, f32[12,512,128]{2,1,0:T(8,128)} %get-tuple-element.262, f32[12,3,512,128]{3,2,1,0:T(8,128)} %get-tuple-element.283, f32[12,512,128]{2,1,0:T(8,128)} %get-tuple-element.263), kind=kLoop, calls=%fused_computation.37.clone.1 | loop fusion | flops 9240576 | bytes 26738688 | tf_op jit(solution)/shard_map/while/body/eval_jaxpr/reduce_sum | solution.py:92
  330.1 5.0 collective-permute-start.3
  336.7 6.5 collective-permute-start.4
  356.2 4.2 fusion.29
  363.3 4.9 collective-permute-done.2
  368.9 11.8 %fusion.30 = (f32[3,512,128]{2,1,0:T(8,128)S(1)}, f32[12,3,512,128]{3,2,1,0:T(8,128)}) fusion(f32[3,512,128]{2,1,0:T(8,128)S(1)} %pad_maximum_fusion.5, f32[12,512,128]{2,1,0:T(8,128)} %get-tuple-element.262, f32[12,3,512,128]{3,2,1,0:T(8,128)} %get-tuple-element.283, f32[12,512,128]{2,1,0:T(8,128)} %get-tuple-element.263), kind=kLoop, calls=%fused_computation.37.clone.1 | loop fusion | flops 9240576 | bytes 26738688 | tf_op jit(solution)/shard_map/while/body/eval_jaxpr/reduce_sum | solution.py:92
  381.2 5.7 collective-permute-start.3
  388.5 6.6 collective-permute-start.4
  408.0 4.2 fusion.29
  415.0 5.0 collective-permute-done.2
  420.7 11.8 %fusion.30 = (f32[3,512,128]{2,1,0:T(8,128)S(1)}, f32[12,3,512,128]{3,2,1,0:T(8,128)}) fusion(f32[3,512,128]{2,1,0:T(8,128)S(1)} %pad_maximum_fusion.5, f32[12,512,128]{2,1,0:T(8,128)} %get-tuple-element.262, f32[12,3,512,128]{3,2,1,0:T(8,128)} %get-tuple-element.283, f32[12,512,128]{2,1,0:T(8,128)} %get-tuple-element.263), kind=kLoop, calls=%fused_computation.37.clone.1 | loop fusion | flops 9240576 | bytes 26738688 | tf_op jit(solution)/shard_map/while/body/eval_jaxpr/reduce_sum | solution.py:92
  433.0 5.7 collective-permute-start.3
  440.3 6.6 collective-permute-start.4
  459.9 4.2 fusion.29
  466.9 5.0 collective-permute-done.2
  472.6 11.8 %fusion.30 = (f32[3,512,128]{2,1,0:T(8,128)S(1)}, f32[12,3,512,128]{3,2,1,0:T(8,128)}) fusion(f32[3,512,128]{2,1,0:T(8,128)S(1)} %pad_maximum_fusion.5, f32[12,512,128]{2,1,0:T(8,128)} %get-tuple-element.262, f32[12,3,512,128]{3,2,1,0:T(8,128)} %get-tuple-element.283, f32[12,512,128]{2,1,0:T(8,128)} %get-tuple-element.263), kind=kLoop, calls=%fused_computation.37.clone.1 | loop fusion | flops 9240576 | bytes 26738688 | tf_op jit(solution)/shard_map/while/body/eval_jaxpr/reduce_sum | solution.py:92
  484.9 5.7 collective-permute-start.3
  492.2 6.6 collective-permute-start.4
  498.8 3.4 collective-permute-start.5
  511.7 4.2 fusion.29
  518.7 5.0 collective-permute-done.2
  524.4 11.8 %fusion.30 = (f32[3,512,128]{2,1,0:T(8,128)S(1)}, f32[12,3,512,128]{3,2,1,0:T(8,128)}) fusion(f32[3,512,128]{2,1,0:T(8,128)S(1)} %pad_maximum_fusion.5, f32[12,512,128]{2,1,0:T(8,128)} %get-tuple-element.262, f32[12,3,512,128]{3,2,1,0:T(8,128)} %get-tuple-element.283, f32[12,512,128]{2,1,0:T(8,128)} %get-tuple-element.263), kind=kLoop, calls=%fused_computation.37.clone.1 | loop fusion | flops 9240576 | bytes 26738688 | tf_op jit(solution)/shard_map/while/body/eval_jaxpr/reduce_sum | solution.py:92
  536.7 5.7 collective-permute-start.3
  544.0 6.6 collective-permute-start.4
  563.6 4.2 fusion.29
  570.6 5.0 collective-permute-done.2
  576.3 11.8 %fusion.30 = (f32[3,512,128]{2,1,0:T(8,128)S(1)}, f32[12,3,512,128]{3,2,1,0:T(8,128)}) fusion(f32[3,512,128]{2,1,0:T(8,128)S(1)} %pad_maximum_fusion.5, f32[12,512,128]{2,1,0:T(8,128)} %get-tuple-element.262, f32[12,3,512,128]{3,2,1,0:T(8,128)} %get-tuple-element.283, f32[12,512,128]{2,1,0:T(8,128)} %get-tuple-element.263), kind=kLoop, calls=%fused_computation.37.clone.1 | loop fusion | flops 9240576 | bytes 26738688 | tf_op jit(solution)/shard_map/while/body/eval_jaxpr/reduce_sum | solution.py:92
  588.6 5.7 collective-permute-start.3
  595.9 6.6 collective-permute-start.4
  615.4 4.2 fusion.29
  622.4 5.0 collective-permute-done.2
  628.1 11.8 %fusion.30 = (f32[3,512,128]{2,1,0:T(8,128)S(1)}, f32[12,3,512,128]{3,2,1,0:T(8,128)}) fusion(f32[3,512,128]{2,1,0:T(8,128)S(1)} %pad_maximum_fusion.5, f32[12,512,128]{2,1,0:T(8,128)} %get-tuple-element.262, f32[12,3,512,128]{3,2,1,0:T(8,128)} %get-tuple-element.283, f32[12,512,128]{2,1,0:T(8,128)} %get-tuple-element.263), kind=kLoop, calls=%fused_computation.37.clone.1 | loop fusion | flops 9240576 | bytes 26738688 | tf_op jit(solution)/shard_map/while/body/eval_jaxpr/reduce_sum | solution.py:92
  640.4 5.7 collective-permute-start.3
  647.7 6.6 collective-permute-start.4
  667.3 4.2 fusion.29
  674.3 5.0 collective-permute-done.2
  680.0 11.8 %fusion.30 = (f32[3,512,128]{2,1,0:T(8,128)S(1)}, f32[12,3,512,128]{3,2,1,0:T(8,128)}) fusion(f32[3,512,128]{2,1,0:T(8,128)S(1)} %pad_maximum_fusion.5, f32[12,512,128]{2,1,0:T(8,128)} %get-tuple-element.262, f32[12,3,512,128]{3,2,1,0:T(8,128)} %get-tuple-element.283, f32[12,512,128]{2,1,0:T(8,128)} %get-tuple-element.263), kind=kLoop, calls=%fused_computation.37.clone.1 | loop fusion | flops 9240576 | bytes 26738688 | tf_op jit(solution)/shard_map/while/body/eval_jaxpr/reduce_sum | solution.py:92
  692.3 5.7 collective-permute-start.3
  699.6 6.6 collective-permute-start.4
  719.1 4.2 fusion.29
  726.1 5.0 collective-permute-done.2
  731.8 11.8 %fusion.30 = (f32[3,512,128]{2,1,0:T(8,128)S(1)}, f32[12,3,512,128]{3,2,1,0:T(8,128)}) fusion(f32[3,512,128]{2,1,0:T(8,128)S(1)} %pad_maximum_fusion.5, f32[12,512,128]{2,1,0:T(8,128)} %get-tuple-element.262, f32[12,3,512,128]{3,2,1,0:T(8,128)} %get-tuple-element.283, f32[12,512,128]{2,1,0:T(8,128)} %get-tuple-element.263), kind=kLoop, calls=%fused_computation.37.clone.1 | loop fusion | flops 9240576 | bytes 26738688 | tf_op jit(solution)/shard_map/while/body/eval_jaxpr/reduce_sum | solution.py:92
  744.1 5.7 collective-permute-start.3
  751.4 6.6 collective-permute-start.4
  (322 shorter events, 183.9 us)
Async XLA Ops:
  0.6 8.6 %copy-start.3 = (f32[512,128]{1,0:T(8,128)S(1)}, f32[512,128]{1,0:T(8,128)}, u32[]{:S(2)}) copy-start(f32[512,128]{1,0:T(8,128)} %param.9) | copy-start | bytes 786436
  0.6 9.3 %copy-start.2 = (f32[10,32,2048]{2,1,0:T(8,128)S(1)}, f32[10,32,2048]{2,1,0:T(8,128)}, u32[]{:S(2)}) copy-start(f32[10,32,2048]{2,1,0:T(8,128)} %param.8) | copy-start | bytes 7864324
  135.6 46.7 %all-to-all-start = ((f32[16,1,40960]{2,1,0:T(1,128)}), f32[16,1,40960]{2,1,0:T(1,128)S(1)}, u32[]{:S(2)}, u32[]{:S(2)}) async-start(f32[16,1,40960]{2,1,0:T(1,128)} %reshape.35), calls=%async_computation | async-start | bytes 5242880 | tf_op jit(solution)/shard_map/all_to_all | solution.py:70
  239.8 3.7 copy-start.5
  243.8 16.1 %collective-permute-start = (f32[2,1,128]{2,1,0:T(1,128)S(1)}, f32[2,1,128]{2,1,0:T(1,128)S(1)}, u32[]{:S(2)}, u32[]{:S(2)}) collective-permute-start(f32[2,1,128]{2,1,0:T(1,128)S(1)} %slice.201), channel_id=1, source_target_pairs={{16,0},{32,16},{48,32},{64,48},{80,64},{96,80},{112,96},{17,1},{33... | collective-permute-start | bytes 3080 | tf_op jit(solution)/shard_map/while/body/eval_jaxpr/ppermute | solution.py:15
  248.5 13.7 %collective-permute-start.1 = (f32[2,512]{1,0:T(2,128)S(1)}, f32[2,512]{1,0:T(2,128)S(1)}, u32[]{:S(2)}, u32[]{:S(2)}) collective-permute-start(f32[2,512]{1,0:T(2,128)S(1)} %slice_reduce_fusion.6), channel_id=1, source_target_pairs={{1,0},{2,1},{3,2},{4,3},{5,4},{6,5},{7,6},{8,7},{9,8},{10,9},{11,1... | collective-permute-start | bytes 12296 | tf_op jit(solution)/shard_map/while/body/eval_jaxpr/ppermute | solution.py:15
  260.2 7.3 collective-permute-start.2
  280.5 5.9 collective-permute-start.3
  287.2 6.1 collective-permute-start.4
  291.4 6.4 collective-permute-start.5
  298.3 11.2 %collective-permute-start = (f32[2,1,128]{2,1,0:T(1,128)S(1)}, f32[2,1,128]{2,1,0:T(1,128)S(1)}, u32[]{:S(2)}, u32[]{:S(2)}) collective-permute-start(f32[2,1,128]{2,1,0:T(1,128)S(1)} %slice.201), channel_id=1, source_target_pairs={{16,0},{32,16},{48,32},{64,48},{80,64},{96,80},{112,96},{17,1},{33... | collective-permute-start | bytes 3080 | tf_op jit(solution)/shard_map/while/body/eval_jaxpr/ppermute | solution.py:15
  300.4 12.6 %collective-permute-start.1 = (f32[2,512]{1,0:T(2,128)S(1)}, f32[2,512]{1,0:T(2,128)S(1)}, u32[]{:S(2)}, u32[]{:S(2)}) collective-permute-start(f32[2,512]{1,0:T(2,128)S(1)} %slice_reduce_fusion.6), channel_id=1, source_target_pairs={{1,0},{2,1},{3,2},{4,3},{5,4},{6,5},{7,6},{8,7},{9,8},{10,9},{11,1... | collective-permute-start | bytes 12296 | tf_op jit(solution)/shard_map/while/body/eval_jaxpr/ppermute | solution.py:15
  309.7 7.3 collective-permute-start.2
  330.1 5.9 collective-permute-start.3
  336.7 9.9 %collective-permute-start.4 = (f32[2,512]{1,0:T(2,128)S(1)}, f32[2,512]{1,0:T(2,128)S(1)}, u32[]{:S(2)}, u32[]{:S(2)}) collective-permute-start(f32[2,512]{1,0:T(2,128)S(1)} %slice_reduce_fusion.8), channel_id=1, source_target_pairs={{0,1},{1,2},{2,3},{3,4},{4,5},{5,6},{6,7},{7,8},{8,9},{9,10},{10,1... | collective-permute-start | bytes 12296 | tf_op jit(solution)/shard_map/while/body/eval_jaxpr/ppermute | solution.py:15
  343.2 6.4 collective-permute-start.5
  350.1 10.5 %collective-permute-start = (f32[2,1,128]{2,1,0:T(1,128)S(1)}, f32[2,1,128]{2,1,0:T(1,128)S(1)}, u32[]{:S(2)}, u32[]{:S(2)}) collective-permute-start(f32[2,1,128]{2,1,0:T(1,128)S(1)} %slice.201), channel_id=1, source_target_pairs={{16,0},{32,16},{48,32},{64,48},{80,64},{96,80},{112,96},{17,1},{33... | collective-permute-start | bytes 3080 | tf_op jit(solution)/shard_map/while/body/eval_jaxpr/ppermute | solution.py:15
  352.3 10.8 %collective-permute-start.1 = (f32[2,512]{1,0:T(2,128)S(1)}, f32[2,512]{1,0:T(2,128)S(1)}, u32[]{:S(2)}, u32[]{:S(2)}) collective-permute-start(f32[2,512]{1,0:T(2,128)S(1)} %slice_reduce_fusion.6), channel_id=1, source_target_pairs={{1,0},{2,1},{3,2},{4,3},{5,4},{6,5},{7,6},{8,7},{9,8},{10,9},{11,1... | collective-permute-start | bytes 12296 | tf_op jit(solution)/shard_map/while/body/eval_jaxpr/ppermute | solution.py:15
  360.8 7.3 collective-permute-start.2
  381.2 6.5 collective-permute-start.3
  388.5 10.0 %collective-permute-start.4 = (f32[2,512]{1,0:T(2,128)S(1)}, f32[2,512]{1,0:T(2,128)S(1)}, u32[]{:S(2)}, u32[]{:S(2)}) collective-permute-start(f32[2,512]{1,0:T(2,128)S(1)} %slice_reduce_fusion.8), channel_id=1, source_target_pairs={{0,1},{1,2},{2,3},{3,4},{4,5},{5,6},{6,7},{7,8},{8,9},{9,10},{10,1... | collective-permute-start | bytes 12296 | tf_op jit(solution)/shard_map/while/body/eval_jaxpr/ppermute | solution.py:15
  395.1 6.4 collective-permute-start.5
  402.0 10.5 %collective-permute-start = (f32[2,1,128]{2,1,0:T(1,128)S(1)}, f32[2,1,128]{2,1,0:T(1,128)S(1)}, u32[]{:S(2)}, u32[]{:S(2)}) collective-permute-start(f32[2,1,128]{2,1,0:T(1,128)S(1)} %slice.201), channel_id=1, source_target_pairs={{16,0},{32,16},{48,32},{64,48},{80,64},{96,80},{112,96},{17,1},{33... | collective-permute-start | bytes 3080 | tf_op jit(solution)/shard_map/while/body/eval_jaxpr/ppermute | solution.py:15
  404.1 10.7 %collective-permute-start.1 = (f32[2,512]{1,0:T(2,128)S(1)}, f32[2,512]{1,0:T(2,128)S(1)}, u32[]{:S(2)}, u32[]{:S(2)}) collective-permute-start(f32[2,512]{1,0:T(2,128)S(1)} %slice_reduce_fusion.6), channel_id=1, source_target_pairs={{1,0},{2,1},{3,2},{4,3},{5,4},{6,5},{7,6},{8,7},{9,8},{10,9},{11,1... | collective-permute-start | bytes 12296 | tf_op jit(solution)/shard_map/while/body/eval_jaxpr/ppermute | solution.py:15
  412.7 7.3 collective-permute-start.2
  433.0 6.5 collective-permute-start.3
  440.3 10.0 %collective-permute-start.4 = (f32[2,512]{1,0:T(2,128)S(1)}, f32[2,512]{1,0:T(2,128)S(1)}, u32[]{:S(2)}, u32[]{:S(2)}) collective-permute-start(f32[2,512]{1,0:T(2,128)S(1)} %slice_reduce_fusion.8), channel_id=1, source_target_pairs={{0,1},{1,2},{2,3},{3,4},{4,5},{5,6},{6,7},{7,8},{8,9},{9,10},{10,1... | collective-permute-start | bytes 12296 | tf_op jit(solution)/shard_map/while/body/eval_jaxpr/ppermute | solution.py:15
  446.9 6.4 collective-permute-start.5
  453.8 10.5 %collective-permute-start = (f32[2,1,128]{2,1,0:T(1,128)S(1)}, f32[2,1,128]{2,1,0:T(1,128)S(1)}, u32[]{:S(2)}, u32[]{:S(2)}) collective-permute-start(f32[2,1,128]{2,1,0:T(1,128)S(1)} %slice.201), channel_id=1, source_target_pairs={{16,0},{32,16},{48,32},{64,48},{80,64},{96,80},{112,96},{17,1},{33... | collective-permute-start | bytes 3080 | tf_op jit(solution)/shard_map/while/body/eval_jaxpr/ppermute | solution.py:15
  456.0 10.7 %collective-permute-start.1 = (f32[2,512]{1,0:T(2,128)S(1)}, f32[2,512]{1,0:T(2,128)S(1)}, u32[]{:S(2)}, u32[]{:S(2)}) collective-permute-start(f32[2,512]{1,0:T(2,128)S(1)} %slice_reduce_fusion.6), channel_id=1, source_target_pairs={{1,0},{2,1},{3,2},{4,3},{5,4},{6,5},{7,6},{8,7},{9,8},{10,9},{11,1... | collective-permute-start | bytes 12296 | tf_op jit(solution)/shard_map/while/body/eval_jaxpr/ppermute | solution.py:15
  464.5 7.3 collective-permute-start.2
  484.9 6.5 collective-permute-start.3
  492.2 10.0 %collective-permute-start.4 = (f32[2,512]{1,0:T(2,128)S(1)}, f32[2,512]{1,0:T(2,128)S(1)}, u32[]{:S(2)}, u32[]{:S(2)}) collective-permute-start(f32[2,512]{1,0:T(2,128)S(1)} %slice_reduce_fusion.8), channel_id=1, source_target_pairs={{0,1},{1,2},{2,3},{3,4},{4,5},{5,6},{6,7},{7,8},{8,9},{9,10},{10,1... | collective-permute-start | bytes 12296 | tf_op jit(solution)/shard_map/while/body/eval_jaxpr/ppermute | solution.py:15
  498.8 6.4 collective-permute-start.5
  505.7 10.5 %collective-permute-start = (f32[2,1,128]{2,1,0:T(1,128)S(1)}, f32[2,1,128]{2,1,0:T(1,128)S(1)}, u32[]{:S(2)}, u32[]{:S(2)}) collective-permute-start(f32[2,1,128]{2,1,0:T(1,128)S(1)} %slice.201), channel_id=1, source_target_pairs={{16,0},{32,16},{48,32},{64,48},{80,64},{96,80},{112,96},{17,1},{33... | collective-permute-start | bytes 3080 | tf_op jit(solution)/shard_map/while/body/eval_jaxpr/ppermute | solution.py:15
  507.8 10.7 %collective-permute-start.1 = (f32[2,512]{1,0:T(2,128)S(1)}, f32[2,512]{1,0:T(2,128)S(1)}, u32[]{:S(2)}, u32[]{:S(2)}) collective-permute-start(f32[2,512]{1,0:T(2,128)S(1)} %slice_reduce_fusion.6), channel_id=1, source_target_pairs={{1,0},{2,1},{3,2},{4,3},{5,4},{6,5},{7,6},{8,7},{9,8},{10,9},{11,1... | collective-permute-start | bytes 12296 | tf_op jit(solution)/shard_map/while/body/eval_jaxpr/ppermute | solution.py:15
  516.4 7.3 collective-permute-start.2
  536.7 6.5 collective-permute-start.3
  544.0 10.0 %collective-permute-start.4 = (f32[2,512]{1,0:T(2,128)S(1)}, f32[2,512]{1,0:T(2,128)S(1)}, u32[]{:S(2)}, u32[]{:S(2)}) collective-permute-start(f32[2,512]{1,0:T(2,128)S(1)} %slice_reduce_fusion.8), channel_id=1, source_target_pairs={{0,1},{1,2},{2,3},{3,4},{4,5},{5,6},{6,7},{7,8},{8,9},{9,10},{10,1... | collective-permute-start | bytes 12296 | tf_op jit(solution)/shard_map/while/body/eval_jaxpr/ppermute | solution.py:15
  550.6 6.4 collective-permute-start.5
  557.5 10.5 %collective-permute-start = (f32[2,1,128]{2,1,0:T(1,128)S(1)}, f32[2,1,128]{2,1,0:T(1,128)S(1)}, u32[]{:S(2)}, u32[]{:S(2)}) collective-permute-start(f32[2,1,128]{2,1,0:T(1,128)S(1)} %slice.201), channel_id=1, source_target_pairs={{16,0},{32,16},{48,32},{64,48},{80,64},{96,80},{112,96},{17,1},{33... | collective-permute-start | bytes 3080 | tf_op jit(solution)/shard_map/while/body/eval_jaxpr/ppermute | solution.py:15
  559.7 10.7 %collective-permute-start.1 = (f32[2,512]{1,0:T(2,128)S(1)}, f32[2,512]{1,0:T(2,128)S(1)}, u32[]{:S(2)}, u32[]{:S(2)}) collective-permute-start(f32[2,512]{1,0:T(2,128)S(1)} %slice_reduce_fusion.6), channel_id=1, source_target_pairs={{1,0},{2,1},{3,2},{4,3},{5,4},{6,5},{7,6},{8,7},{9,8},{10,9},{11,1... | collective-permute-start | bytes 12296 | tf_op jit(solution)/shard_map/while/body/eval_jaxpr/ppermute | solution.py:15
  568.2 7.3 collective-permute-start.2
  588.6 6.5 collective-permute-start.3
  595.9 10.0 %collective-permute-start.4 = (f32[2,512]{1,0:T(2,128)S(1)}, f32[2,512]{1,0:T(2,128)S(1)}, u32[]{:S(2)}, u32[]{:S(2)}) collective-permute-start(f32[2,512]{1,0:T(2,128)S(1)} %slice_reduce_fusion.8), channel_id=1, source_target_pairs={{0,1},{1,2},{2,3},{3,4},{4,5},{5,6},{6,7},{7,8},{8,9},{9,10},{10,1... | collective-permute-start | bytes 12296 | tf_op jit(solution)/shard_map/while/body/eval_jaxpr/ppermute | solution.py:15
  602.5 6.4 collective-permute-start.5
  609.4 10.5 %collective-permute-start = (f32[2,1,128]{2,1,0:T(1,128)S(1)}, f32[2,1,128]{2,1,0:T(1,128)S(1)}, u32[]{:S(2)}, u32[]{:S(2)}) collective-permute-start(f32[2,1,128]{2,1,0:T(1,128)S(1)} %slice.201), channel_id=1, source_target_pairs={{16,0},{32,16},{48,32},{64,48},{80,64},{96,80},{112,96},{17,1},{33... | collective-permute-start | bytes 3080 | tf_op jit(solution)/shard_map/while/body/eval_jaxpr/ppermute | solution.py:15
  611.5 10.7 %collective-permute-start.1 = (f32[2,512]{1,0:T(2,128)S(1)}, f32[2,512]{1,0:T(2,128)S(1)}, u32[]{:S(2)}, u32[]{:S(2)}) collective-permute-start(f32[2,512]{1,0:T(2,128)S(1)} %slice_reduce_fusion.6), channel_id=1, source_target_pairs={{1,0},{2,1},{3,2},{4,3},{5,4},{6,5},{7,6},{8,7},{9,8},{10,9},{11,1... | collective-permute-start | bytes 12296 | tf_op jit(solution)/shard_map/while/body/eval_jaxpr/ppermute | solution.py:15
  620.1 7.3 collective-permute-start.2
  640.4 6.5 collective-permute-start.3
  647.7 10.0 %collective-permute-start.4 = (f32[2,512]{1,0:T(2,128)S(1)}, f32[2,512]{1,0:T(2,128)S(1)}, u32[]{:S(2)}, u32[]{:S(2)}) collective-permute-start(f32[2,512]{1,0:T(2,128)S(1)} %slice_reduce_fusion.8), channel_id=1, source_target_pairs={{0,1},{1,2},{2,3},{3,4},{4,5},{5,6},{6,7},{7,8},{8,9},{9,10},{10,1... | collective-permute-start | bytes 12296 | tf_op jit(solution)/shard_map/while/body/eval_jaxpr/ppermute | solution.py:15
  654.3 6.4 collective-permute-start.5
  661.2 10.5 %collective-permute-start = (f32[2,1,128]{2,1,0:T(1,128)S(1)}, f32[2,1,128]{2,1,0:T(1,128)S(1)}, u32[]{:S(2)}, u32[]{:S(2)}) collective-permute-start(f32[2,1,128]{2,1,0:T(1,128)S(1)} %slice.201), channel_id=1, source_target_pairs={{16,0},{32,16},{48,32},{64,48},{80,64},{96,80},{112,96},{17,1},{33... | collective-permute-start | bytes 3080 | tf_op jit(solution)/shard_map/while/body/eval_jaxpr/ppermute | solution.py:15
  663.4 10.7 %collective-permute-start.1 = (f32[2,512]{1,0:T(2,128)S(1)}, f32[2,512]{1,0:T(2,128)S(1)}, u32[]{:S(2)}, u32[]{:S(2)}) collective-permute-start(f32[2,512]{1,0:T(2,128)S(1)} %slice_reduce_fusion.6), channel_id=1, source_target_pairs={{1,0},{2,1},{3,2},{4,3},{5,4},{6,5},{7,6},{8,7},{9,8},{10,9},{11,1... | collective-permute-start | bytes 12296 | tf_op jit(solution)/shard_map/while/body/eval_jaxpr/ppermute | solution.py:15
  671.9 7.3 collective-permute-start.2
  692.3 6.5 collective-permute-start.3
  699.6 10.0 %collective-permute-start.4 = (f32[2,512]{1,0:T(2,128)S(1)}, f32[2,512]{1,0:T(2,128)S(1)}, u32[]{:S(2)}, u32[]{:S(2)}) collective-permute-start(f32[2,512]{1,0:T(2,128)S(1)} %slice_reduce_fusion.8), channel_id=1, source_target_pairs={{0,1},{1,2},{2,3},{3,4},{4,5},{5,6},{6,7},{7,8},{8,9},{9,10},{10,1... | collective-permute-start | bytes 12296 | tf_op jit(solution)/shard_map/while/body/eval_jaxpr/ppermute | solution.py:15
  706.2 6.4 collective-permute-start.5
  713.1 10.5 %collective-permute-start = (f32[2,1,128]{2,1,0:T(1,128)S(1)}, f32[2,1,128]{2,1,0:T(1,128)S(1)}, u32[]{:S(2)}, u32[]{:S(2)}) collective-permute-start(f32[2,1,128]{2,1,0:T(1,128)S(1)} %slice.201), channel_id=1, source_target_pairs={{16,0},{32,16},{48,32},{64,48},{80,64},{96,80},{112,96},{17,1},{33... | collective-permute-start | bytes 3080 | tf_op jit(solution)/shard_map/while/body/eval_jaxpr/ppermute | solution.py:15
  715.2 10.7 %collective-permute-start.1 = (f32[2,512]{1,0:T(2,128)S(1)}, f32[2,512]{1,0:T(2,128)S(1)}, u32[]{:S(2)}, u32[]{:S(2)}) collective-permute-start(f32[2,512]{1,0:T(2,128)S(1)} %slice_reduce_fusion.6), channel_id=1, source_target_pairs={{1,0},{2,1},{3,2},{4,3},{5,4},{6,5},{7,6},{8,7},{9,8},{10,9},{11,1... | collective-permute-start | bytes 12296 | tf_op jit(solution)/shard_map/while/body/eval_jaxpr/ppermute | solution.py:15
  723.8 7.3 collective-permute-start.2
  744.1 6.5 collective-permute-start.3
  751.4 10.0 %collective-permute-start.4 = (f32[2,512]{1,0:T(2,128)S(1)}, f32[2,512]{1,0:T(2,128)S(1)}, u32[]{:S(2)}, u32[]{:S(2)}) collective-permute-start(f32[2,512]{1,0:T(2,128)S(1)} %slice_reduce_fusion.8), channel_id=1, source_target_pairs={{0,1},{1,2},{2,3},{3,4},{4,5},{5,6},{6,7},{7,8},{8,9},{9,10},{10,1... | collective-permute-start | bytes 12296 | tf_op jit(solution)/shard_map/while/body/eval_jaxpr/ppermute | solution.py:15
  758.0 6.4 collective-permute-start.5
  (3 other events, 8.2 us)
where the time goes:
time: 769 us; the launch traced here: 766 us
  other arithmetic  304 us (40%)
  starting transfers between devices  222 us (29%)
  waiting for transfers between devices  127 us (17%)
  local copies, waits for them, and re-layouts  111 us (14%)
    ppermute x60, starting transfers between devices, shifted(): return lax.ppermute(shard, axis, pairs)  214 us
    reduce_sum x10, other arithmetic, march_forward(): stress = jnp.sum(mode_next, axis=0)  118 us
    unnamed x1, other arithmetic  94.9 us
    ppermute x60, waiting for transfers between devices, shifted(): return lax.ppermute(shard, axis, pairs)  87.9 us
    unnamed x17, local copies, waits for them, and re-layouts  49.7 us
    exp x10, other arithmetic, relax_mode(): kept = jnp.exp(-rate_ratio)  41.8 us
    all_to_all x1, waiting for transfers between devices, shards(): lax.all_to_all(sheet_pieces, ('width', 'cores'), split_axis=3, concat_axi...  39.1 us
    all_to_all x2, local copies, waits for them, and re-layouts, shards(): lax.all_to_all(sheet_pieces, ('width', 'cores'), split_axis=3, concat_axi...  24.4 us
  transfers between devices with their start and end apart: 61, of which 31 were waited for; matrix products, arithmetic and copies ran while one was open for 10% of the time, Pallas kernels for 0%

commit v1 on v0

--- a/solution.py
+++ b/solution.py
@@ -67,8 +67,14 @@
     row_count = vertex_velocity.shape[1]
     col_count = vertex_velocity.shape[2]
     sheet_pieces = warmth_history.reshape(tick_ordinal, 1, piece_lines, entire_breadth)
-    arrived_block = lax.all_to_all(
-        sheet_pieces, ("width", "cores"), split_axis=3, concat_axis=1, tiled=True
+    arrived_block = jnp.concatenate(
+        lax.all_to_all(
+            jnp.stack(jnp.split(sheet_pieces, lax.axis_size(("width", "cores")), axis=3)),
+            ("width", "cores"),
+            0,
+            0,
+        ),
+        axis=1,
     )
     heat_all, term_all = heat_terms(
         arrived_block.reshape(arrived_block.shape[0], row_count, col_count)

time: 769 us -> 598 us (0.78)
  other arithmetic: 304 us -> 200 us
  local copies, waits for them, and re-layouts: 111 us -> 45.3 us
    unnamed x1 -> x0, other arithmetic: 94.9 us -> none
    unnamed x17 -> x27, local copies, waits for them, and re-layouts: 49.7 us -> 21.4 us
    all_to_all x2 -> x0, local copies, waits for them, and re-layouts: 24.4 us -> none  [shards(): lax.all_to_all(sheet_pieces, ('width', 'cores'), split_axis=3, concat_axi...]
    reshape x1, local copies, waits for them, and re-layouts: 15.1 us -> 1.88 us  [shards(): jnp.concatenate(lax.all_to_all(jnp.stack(jnp.split(sheet_pieces, lax.axis...]
    all_to_all x1 -> x0, other arithmetic: 9.18 us -> none  [shards(): lax.all_to_all(sheet_pieces, ('width', 'cores'), split_axis=3, concat_axi...]
  transfers between devices with their start and end apart: 61 -> 61, of which waited for: 31 -> 31; matrix products, arithmetic and copies ran while one was open for 10% -> 13% of each run, Pallas kernels for 0% -> 0%
where the time goes in v1:
time: 598 us; the launch traced here: 596 us
  starting transfers between devices  222 us (37%)
  other arithmetic  200 us (33%)
  waiting for transfers between devices  127 us (21%)
  local copies, waits for them, and re-layouts  45.3 us (8%)
    ppermute x60, starting transfers between devices, shifted(): return lax.ppermute(shard, axis, pairs)  214 us
    reduce_sum x10, other arithmetic, march_forward(): stress = jnp.sum(mode_next, axis=0)  118 us
    ppermute x60, waiting for transfers between devices, shifted(): return lax.ppermute(shard, axis, pairs)  87.9 us
    exp x10, other arithmetic, relax_mode(): kept = jnp.exp(-rate_ratio)  41.9 us
    all_to_all x1, waiting for transfers between devices, shards(): lax.all_to_all(jnp.stack(jnp.split(sheet_pieces, lax.axis_size(('width',...  39.1 us
    unnamed x27, local copies, waits for them, and re-layouts  21.4 us
    exp x10, other arithmetic, march_forward(): jnp.exp(warming_contribution + arrhenius_energy * (1.0 - coupling_exponen...  19.8 us
  transfers between devices with their start and end apart: 61, of which 31 were waited for; matrix products, arithmetic and copies ran while one was open for 13% of the time, Pallas kernels for 0%

profile of v1, /device:TPU:97, one launch (start us, length us, event | category | flops | bytes accessed | tf_op | source)
XLA Modules:
  0.0 596.3 jit_solution(2815262359173280867)
XLA Ops:
  2.3 8.6 %copy.68 = f32[12,3,512,128]{3,2,1,0:T(8,128)} copy(f32[12,3,512,128]{3,2,1,0:T(8,128)} %param.11) | data formatting | bytes 18874368
  21.9 7.6 %all-to-all-start = ((f32[16,10,1,32,128]{4,3,1,2,0:T(8,128)}), f32[16,10,1,32,128]{4,3,1,2,0:T(8,128)S(1)}, u32[]{:S(2)}, u32[]{:S(2)}) async-start(f32[16,10,1,32,128]{4,3,1,2,0:T(8,128)} %fusion.13), calls=%async_computation | async-start | bytes 5242880 | tf_op jit(solution)/shard_map/all_to_all | solution.py:71
  29.5 39.1 %all-to-all-done = f32[16,10,1,32,128]{4,3,1,2,0:T(8,128)S(1)} async-done(((f32[16,10,1,32,128]{4,3,1,2,0:T(8,128)}), f32[16,10,1,32,128]{4,3,1,2,0:T(8,128)S(1)}, u32[]{:S(2)}, u32[]{:S(2)}) %all-to-all-start) | async-done | bytes 2621472 | tf_op jit(solution)/shard_map/all_to_all | solution.py:71
  70.5 3.7 divide_add_fusion
  74.3 521.2 %while.17 = (s32[]{:T(128)}, f32[512,128]{1,0:T(8,128)}, f32[2,512,128]{2,1,0:T(8,128)S(1)}, f32[12,3,512,128]{3,2,1,0:T(8,128)}, f32[10,512,128]{2,1,0:T(8,128)...) while((s32[]{:T(128)}, f32[512,128]{1,0:T(8,128)}, ...), condition=%wide.region_2.3_spmd, body=%wide.region_0.2_spmd.sunk | while | flops 19660812 | bytes 53078544 | solution.py:102
  74.3 4.5 collective-permute-start
  79.0 5.0 collective-permute-start.1
  85.9 4.2 fusion.45
  93.0 5.0 collective-permute-done.2
  98.6 11.8 %fusion.46 = (f32[3,512,128]{2,1,0:T(8,128)S(1)}, f32[12,3,512,128]{3,2,1,0:T(8,128)}) fusion(f32[3,512,128]{2,1,0:T(8,128)S(1)} %pad_maximum_fusion.5, f32[12,512,128]{2,1,0:T(8,128)} %get-tuple-element.262, f32[12,3,512,128]{3,2,1,0:T(8,128)} %get-tuple-element.283, f32[12,512,128]{2,1,0:T(8,128)} %get-tuple-element.263), kind=kLoop, calls=%fused_computation.69.clone.1 | loop fusion | flops 9240576 | bytes 26738688 | tf_op jit(solution)/shard_map/while/body/eval_jaxpr/reduce_sum | solution.py:98
  117.6 4.1 collective-permute-start.4
  124.0 4.3 collective-permute-done.5
  135.5 4.2 fusion.45
  143.7 3.8 collective-permute-done.2
  148.2 11.8 %fusion.46 = (f32[3,512,128]{2,1,0:T(8,128)S(1)}, f32[12,3,512,128]{3,2,1,0:T(8,128)}) fusion(f32[3,512,128]{2,1,0:T(8,128)S(1)} %pad_maximum_fusion.5, f32[12,512,128]{2,1,0:T(8,128)} %get-tuple-element.262, f32[12,3,512,128]{3,2,1,0:T(8,128)} %get-tuple-element.283, f32[12,512,128]{2,1,0:T(8,128)} %get-tuple-element.263), kind=kLoop, calls=%fused_computation.69.clone.1 | loop fusion | flops 9240576 | bytes 26738688 | tf_op jit(solution)/shard_map/while/body/eval_jaxpr/reduce_sum | solution.py:98
  160.5 5.0 collective-permute-start.3
  167.2 6.5 %collective-permute-start.4 = (f32[2,512]{1,0:T(2,128)S(1)}, f32[2,512]{1,0:T(2,128)S(1)}, u32[]{:S(2)}, u32[]{:S(2)}) collective-permute-start(f32[2,512]{1,0:T(2,128)S(1)} %slice_reduce_fusion.8), channel_id=1, source_target_pairs={{0,1},{1,2},{2,3},{3,4},{4,5},{5,6},{6,7},{7,8},{8,9},{9,10},{10,1... | collective-permute-start | bytes 12296 | tf_op jit(solution)/shard_map/while/body/eval_jaxpr/ppermute | solution.py:15
  173.7 3.4 collective-permute-start.5
  186.6 4.2 fusion.45
  193.8 4.9 collective-permute-done.2
  199.3 11.8 %fusion.46 = (f32[3,512,128]{2,1,0:T(8,128)S(1)}, f32[12,3,512,128]{3,2,1,0:T(8,128)}) fusion(f32[3,512,128]{2,1,0:T(8,128)S(1)} %pad_maximum_fusion.5, f32[12,512,128]{2,1,0:T(8,128)} %get-tuple-element.262, f32[12,3,512,128]{3,2,1,0:T(8,128)} %get-tuple-element.283, f32[12,512,128]{2,1,0:T(8,128)} %get-tuple-element.263), kind=kLoop, calls=%fused_computation.69.clone.1 | loop fusion | flops 9240576 | bytes 26738688 | tf_op jit(solution)/shard_map/while/body/eval_jaxpr/reduce_sum | solution.py:98
  211.7 5.7 collective-permute-start.3
  218.9 6.6 %collective-permute-start.4 = (f32[2,512]{1,0:T(2,128)S(1)}, f32[2,512]{1,0:T(2,128)S(1)}, u32[]{:S(2)}, u32[]{:S(2)}) collective-permute-start(f32[2,512]{1,0:T(2,128)S(1)} %slice_reduce_fusion.8), channel_id=1, source_target_pairs={{0,1},{1,2},{2,3},{3,4},{4,5},{5,6},{6,7},{7,8},{8,9},{9,10},{10,1... | collective-permute-start | bytes 12296 | tf_op jit(solution)/shard_map/while/body/eval_jaxpr/ppermute | solution.py:15
  225.5 3.4 collective-permute-start.5
  238.5 4.2 fusion.45
  245.5 5.0 collective-permute-done.2
  251.2 11.8 %fusion.46 = (f32[3,512,128]{2,1,0:T(8,128)S(1)}, f32[12,3,512,128]{3,2,1,0:T(8,128)}) fusion(f32[3,512,128]{2,1,0:T(8,128)S(1)} %pad_maximum_fusion.5, f32[12,512,128]{2,1,0:T(8,128)} %get-tuple-element.262, f32[12,3,512,128]{3,2,1,0:T(8,128)} %get-tuple-element.283, f32[12,512,128]{2,1,0:T(8,128)} %get-tuple-element.263), kind=kLoop, calls=%fused_computation.69.clone.1 | loop fusion | flops 9240576 | bytes 26738688 | tf_op jit(solution)/shard_map/while/body/eval_jaxpr/reduce_sum | solution.py:98
  263.5 5.7 collective-permute-start.3
  270.8 6.6 %collective-permute-start.4 = (f32[2,512]{1,0:T(2,128)S(1)}, f32[2,512]{1,0:T(2,128)S(1)}, u32[]{:S(2)}, u32[]{:S(2)}) collective-permute-start(f32[2,512]{1,0:T(2,128)S(1)} %slice_reduce_fusion.8), channel_id=1, source_target_pairs={{0,1},{1,2},{2,3},{3,4},{4,5},{5,6},{6,7},{7,8},{8,9},{9,10},{10,1... | collective-permute-start | bytes 12296 | tf_op jit(solution)/shard_map/while/body/eval_jaxpr/ppermute | solution.py:15
  277.4 3.4 collective-permute-start.5
  290.4 4.2 fusion.45
  297.4 5.0 collective-permute-done.2
  303.1 11.8 %fusion.46 = (f32[3,512,128]{2,1,0:T(8,128)S(1)}, f32[12,3,512,128]{3,2,1,0:T(8,128)}) fusion(f32[3,512,128]{2,1,0:T(8,128)S(1)} %pad_maximum_fusion.5, f32[12,512,128]{2,1,0:T(8,128)} %get-tuple-element.262, f32[12,3,512,128]{3,2,1,0:T(8,128)} %get-tuple-element.283, f32[12,512,128]{2,1,0:T(8,128)} %get-tuple-element.263), kind=kLoop, calls=%fused_computation.69.clone.1 | loop fusion | flops 9240576 | bytes 26738688 | tf_op jit(solution)/shard_map/while/body/eval_jaxpr/reduce_sum | solution.py:98
  315.4 5.7 collective-permute-start.3
  322.7 6.6 %collective-permute-start.4 = (f32[2,512]{1,0:T(2,128)S(1)}, f32[2,512]{1,0:T(2,128)S(1)}, u32[]{:S(2)}, u32[]{:S(2)}) collective-permute-start(f32[2,512]{1,0:T(2,128)S(1)} %slice_reduce_fusion.8), channel_id=1, source_target_pairs={{0,1},{1,2},{2,3},{3,4},{4,5},{5,6},{6,7},{7,8},{8,9},{9,10},{10,1... | collective-permute-start | bytes 12296 | tf_op jit(solution)/shard_map/while/body/eval_jaxpr/ppermute | solution.py:15
  329.3 3.4 collective-permute-start.5
  342.2 4.2 fusion.45
  349.2 5.0 collective-permute-done.2
  354.9 11.8 %fusion.46 = (f32[3,512,128]{2,1,0:T(8,128)S(1)}, f32[12,3,512,128]{3,2,1,0:T(8,128)}) fusion(f32[3,512,128]{2,1,0:T(8,128)S(1)} %pad_maximum_fusion.5, f32[12,512,128]{2,1,0:T(8,128)} %get-tuple-element.262, f32[12,3,512,128]{3,2,1,0:T(8,128)} %get-tuple-element.283, f32[12,512,128]{2,1,0:T(8,128)} %get-tuple-element.263), kind=kLoop, calls=%fused_computation.69.clone.1 | loop fusion | flops 9240576 | bytes 26738688 | tf_op jit(solution)/shard_map/while/body/eval_jaxpr/reduce_sum | solution.py:98
  367.2 5.7 collective-permute-start.3
  374.5 6.6 %collective-permute-start.4 = (f32[2,512]{1,0:T(2,128)S(1)}, f32[2,512]{1,0:T(2,128)S(1)}, u32[]{:S(2)}, u32[]{:S(2)}) collective-permute-start(f32[2,512]{1,0:T(2,128)S(1)} %slice_reduce_fusion.8), channel_id=1, source_target_pairs={{0,1},{1,2},{2,3},{3,4},{4,5},{5,6},{6,7},{7,8},{8,9},{9,10},{10,1... | collective-permute-start | bytes 12296 | tf_op jit(solution)/shard_map/while/body/eval_jaxpr/ppermute | solution.py:15
  381.1 3.4 collective-permute-start.5
  394.1 4.2 fusion.45
  401.1 5.0 collective-permute-done.2
  406.8 11.8 %fusion.46 = (f32[3,512,128]{2,1,0:T(8,128)S(1)}, f32[12,3,512,128]{3,2,1,0:T(8,128)}) fusion(f32[3,512,128]{2,1,0:T(8,128)S(1)} %pad_maximum_fusion.5, f32[12,512,128]{2,1,0:T(8,128)} %get-tuple-element.262, f32[12,3,512,128]{3,2,1,0:T(8,128)} %get-tuple-element.283, f32[12,512,128]{2,1,0:T(8,128)} %get-tuple-element.263), kind=kLoop, calls=%fused_computation.69.clone.1 | loop fusion | flops 9240576 | bytes 26738688 | tf_op jit(solution)/shard_map/while/body/eval_jaxpr/reduce_sum | solution.py:98
  419.1 5.7 collective-permute-start.3
  426.4 6.6 %collective-permute-start.4 = (f32[2,512]{1,0:T(2,128)S(1)}, f32[2,512]{1,0:T(2,128)S(1)}, u32[]{:S(2)}, u32[]{:S(2)}) collective-permute-start(f32[2,512]{1,0:T(2,128)S(1)} %slice_reduce_fusion.8), channel_id=1, source_target_pairs={{0,1},{1,2},{2,3},{3,4},{4,5},{5,6},{6,7},{7,8},{8,9},{9,10},{10,1... | collective-permute-start | bytes 12296 | tf_op jit(solution)/shard_map/while/body/eval_jaxpr/ppermute | solution.py:15
  445.9 4.2 fusion.45
  453.0 5.0 collective-permute-done.2
  458.6 11.8 %fusion.46 = (f32[3,512,128]{2,1,0:T(8,128)S(1)}, f32[12,3,512,128]{3,2,1,0:T(8,128)}) fusion(f32[3,512,128]{2,1,0:T(8,128)S(1)} %pad_maximum_fusion.5, f32[12,512,128]{2,1,0:T(8,128)} %get-tuple-element.262, f32[12,3,512,128]{3,2,1,0:T(8,128)} %get-tuple-element.283, f32[12,512,128]{2,1,0:T(8,128)} %get-tuple-element.263), kind=kLoop, calls=%fused_computation.69.clone.1 | loop fusion | flops 9240576 | bytes 26738688 | tf_op jit(solution)/shard_map/while/body/eval_jaxpr/reduce_sum | solution.py:98
  471.0 5.7 collective-permute-start.3
  478.3 6.6 %collective-permute-start.4 = (f32[2,512]{1,0:T(2,128)S(1)}, f32[2,512]{1,0:T(2,128)S(1)}, u32[]{:S(2)}, u32[]{:S(2)}) collective-permute-start(f32[2,512]{1,0:T(2,128)S(1)} %slice_reduce_fusion.8), channel_id=1, source_target_pairs={{0,1},{1,2},{2,3},{3,4},{4,5},{5,6},{6,7},{7,8},{8,9},{9,10},{10,1... | collective-permute-start | bytes 12296 | tf_op jit(solution)/shard_map/while/body/eval_jaxpr/ppermute | solution.py:15
  497.8 4.2 fusion.45
  504.8 5.0 collective-permute-done.2
  510.5 11.8 %fusion.46 = (f32[3,512,128]{2,1,0:T(8,128)S(1)}, f32[12,3,512,128]{3,2,1,0:T(8,128)}) fusion(f32[3,512,128]{2,1,0:T(8,128)S(1)} %pad_maximum_fusion.5, f32[12,512,128]{2,1,0:T(8,128)} %get-tuple-element.262, f32[12,3,512,128]{3,2,1,0:T(8,128)} %get-tuple-element.283, f32[12,512,128]{2,1,0:T(8,128)} %get-tuple-element.263), kind=kLoop, calls=%fused_computation.69.clone.1 | loop fusion | flops 9240576 | bytes 26738688 | tf_op jit(solution)/shard_map/while/body/eval_jaxpr/reduce_sum | solution.py:98
  522.8 5.7 collective-permute-start.3
  530.1 6.6 %collective-permute-start.4 = (f32[2,512]{1,0:T(2,128)S(1)}, f32[2,512]{1,0:T(2,128)S(1)}, u32[]{:S(2)}, u32[]{:S(2)}) collective-permute-start(f32[2,512]{1,0:T(2,128)S(1)} %slice_reduce_fusion.8), channel_id=1, source_target_pairs={{0,1},{1,2},{2,3},{3,4},{4,5},{5,6},{6,7},{7,8},{8,9},{9,10},{10,1... | collective-permute-start | bytes 12296 | tf_op jit(solution)/shard_map/while/body/eval_jaxpr/ppermute | solution.py:15
  536.7 3.4 collective-permute-start.5
  549.7 4.2 fusion.45
  556.7 5.0 collective-permute-done.2
  562.4 11.8 %fusion.46 = (f32[3,512,128]{2,1,0:T(8,128)S(1)}, f32[12,3,512,128]{3,2,1,0:T(8,128)}) fusion(f32[3,512,128]{2,1,0:T(8,128)S(1)} %pad_maximum_fusion.5, f32[12,512,128]{2,1,0:T(8,128)} %get-tuple-element.262, f32[12,3,512,128]{3,2,1,0:T(8,128)} %get-tuple-element.283, f32[12,512,128]{2,1,0:T(8,128)} %get-tuple-element.263), kind=kLoop, calls=%fused_computation.69.clone.1 | loop fusion | flops 9240576 | bytes 26738688 | tf_op jit(solution)/shard_map/while/body/eval_jaxpr/reduce_sum | solution.py:98
  574.7 5.7 collective-permute-start.3
  582.0 6.6 %collective-permute-start.4 = (f32[2,512]{1,0:T(2,128)S(1)}, f32[2,512]{1,0:T(2,128)S(1)}, u32[]{:S(2)}, u32[]{:S(2)}) collective-permute-start(f32[2,512]{1,0:T(2,128)S(1)} %slice_reduce_fusion.8), channel_id=1, source_target_pairs={{0,1},{1,2},{2,3},{3,4},{4,5},{5,6},{6,7},{7,8},{8,9},{9,10},{10,1... | collective-permute-start | bytes 12296 | tf_op jit(solution)/shard_map/while/body/eval_jaxpr/ppermute | solution.py:15
  588.6 3.4 collective-permute-start.5
  (329 shorter events, 174.8 us)
Async XLA Ops:
  2.3 8.6 %copy-start.2 = (f32[10,32,2048]{2,1,0:T(8,128)S(1)}, f32[10,32,2048]{2,1,0:T(8,128)}, u32[]{:S(2)}) copy-start(f32[10,32,2048]{2,1,0:T(8,128)} %param.8) | copy-start | bytes 7864324
  21.9 46.7 %all-to-all-start = ((f32[16,10,1,32,128]{4,3,1,2,0:T(8,128)}), f32[16,10,1,32,128]{4,3,1,2,0:T(8,128)S(1)}, u32[]{:S(2)}, u32[]{:S(2)}) async-start(f32[16,10,1,32,128]{4,3,1,2,0:T(8,128)} %fusion.13), calls=%async_computation | async-start | bytes 5242880 | tf_op jit(solution)/shard_map/all_to_all | solution.py:71
  70.5 3.7 copy-start.3
  70.5 3.7 copy-start.4
  74.3 16.1 %collective-permute-start = (f32[2,1,128]{2,1,0:T(1,128)S(1)}, f32[2,1,128]{2,1,0:T(1,128)S(1)}, u32[]{:S(2)}, u32[]{:S(2)}) collective-permute-start(f32[2,1,128]{2,1,0:T(1,128)S(1)} %slice.201), channel_id=1, source_target_pairs={{16,0},{32,16},{48,32},{64,48},{80,64},{96,80},{112,96},{17,1},{33... | collective-permute-start | bytes 3080 | tf_op jit(solution)/shard_map/while/body/eval_jaxpr/ppermute | solution.py:15
  79.0 13.8 %collective-permute-start.1 = (f32[2,512]{1,0:T(2,128)S(1)}, f32[2,512]{1,0:T(2,128)S(1)}, u32[]{:S(2)}, u32[]{:S(2)}) collective-permute-start(f32[2,512]{1,0:T(2,128)S(1)} %slice_reduce_fusion.6), channel_id=1, source_target_pairs={{1,0},{2,1},{3,2},{4,3},{5,4},{6,5},{7,6},{8,7},{9,8},{10,9},{11,1... | collective-permute-start | bytes 12296 | tf_op jit(solution)/shard_map/while/body/eval_jaxpr/ppermute | solution.py:15
  90.6 7.3 %collective-permute-start.2 = (f32[2,512]{1,0:T(2,128)S(1)}, f32[2,512]{1,0:T(2,128)S(1)}, u32[]{:S(2)}, u32[]{:S(2)}) collective-permute-start(f32[2,512]{1,0:T(2,128)S(1)} %fusion.42), channel_id=1, source_target_pairs={{1,0},{2,1},{3,2},{4,3},{5,4},{6,5},{7,6},{8,7},{9,8},{10,9},{11,1... | collective-permute-start | bytes 12296 | tf_op jit(solution)/shard_map/while/body/eval_jaxpr/ppermute | solution.py:15
  111.0 5.9 collective-permute-start.3
  117.6 6.1 %collective-permute-start.4 = (f32[2,512]{1,0:T(2,128)S(1)}, f32[2,512]{1,0:T(2,128)S(1)}, u32[]{:S(2)}, u32[]{:S(2)}) collective-permute-start(f32[2,512]{1,0:T(2,128)S(1)} %slice_reduce_fusion.8), channel_id=1, source_target_pairs={{0,1},{1,2},{2,3},{3,4},{4,5},{5,6},{6,7},{7,8},{8,9},{9,10},{10,1... | collective-permute-start | bytes 12296 | tf_op jit(solution)/shard_map/while/body/eval_jaxpr/ppermute | solution.py:15
  121.8 6.4 %collective-permute-start.5 = (f32[2,1,128]{2,1,0:T(1,128)S(1)}, f32[2,1,128]{2,1,0:T(1,128)S(1)}, u32[]{:S(2)}, u32[]{:S(2)}) collective-permute-start(f32[2,1,128]{2,1,0:T(1,128)S(1)} %slice.204), channel_id=1, source_target_pairs={{0,16},{16,32},{32,48},{48,64},{64,80},{80,96},{96,112},{1,17},{17... | collective-permute-start | bytes 3080 | tf_op jit(solution)/shard_map/while/body/eval_jaxpr/ppermute | solution.py:15
  128.7 11.2 %collective-permute-start = (f32[2,1,128]{2,1,0:T(1,128)S(1)}, f32[2,1,128]{2,1,0:T(1,128)S(1)}, u32[]{:S(2)}, u32[]{:S(2)}) collective-permute-start(f32[2,1,128]{2,1,0:T(1,128)S(1)} %slice.201), channel_id=1, source_target_pairs={{16,0},{32,16},{48,32},{64,48},{80,64},{96,80},{112,96},{17,1},{33... | collective-permute-start | bytes 3080 | tf_op jit(solution)/shard_map/while/body/eval_jaxpr/ppermute | solution.py:15
  130.8 12.6 %collective-permute-start.1 = (f32[2,512]{1,0:T(2,128)S(1)}, f32[2,512]{1,0:T(2,128)S(1)}, u32[]{:S(2)}, u32[]{:S(2)}) collective-permute-start(f32[2,512]{1,0:T(2,128)S(1)} %slice_reduce_fusion.6), channel_id=1, source_target_pairs={{1,0},{2,1},{3,2},{4,3},{5,4},{6,5},{7,6},{8,7},{9,8},{10,9},{11,1... | collective-permute-start | bytes 12296 | tf_op jit(solution)/shard_map/while/body/eval_jaxpr/ppermute | solution.py:15
  140.1 7.3 %collective-permute-start.2 = (f32[2,512]{1,0:T(2,128)S(1)}, f32[2,512]{1,0:T(2,128)S(1)}, u32[]{:S(2)}, u32[]{:S(2)}) collective-permute-start(f32[2,512]{1,0:T(2,128)S(1)} %fusion.42), channel_id=1, source_target_pairs={{1,0},{2,1},{3,2},{4,3},{5,4},{6,5},{7,6},{8,7},{9,8},{10,9},{11,1... | collective-permute-start | bytes 12296 | tf_op jit(solution)/shard_map/while/body/eval_jaxpr/ppermute | solution.py:15
  160.5 5.9 collective-permute-start.3
  167.2 9.9 %collective-permute-start.4 = (f32[2,512]{1,0:T(2,128)S(1)}, f32[2,512]{1,0:T(2,128)S(1)}, u32[]{:S(2)}, u32[]{:S(2)}) collective-permute-start(f32[2,512]{1,0:T(2,128)S(1)} %slice_reduce_fusion.8), channel_id=1, source_target_pairs={{0,1},{1,2},{2,3},{3,4},{4,5},{5,6},{6,7},{7,8},{8,9},{9,10},{10,1... | collective-permute-start | bytes 12296 | tf_op jit(solution)/shard_map/while/body/eval_jaxpr/ppermute | solution.py:15
  173.7 6.4 %collective-permute-start.5 = (f32[2,1,128]{2,1,0:T(1,128)S(1)}, f32[2,1,128]{2,1,0:T(1,128)S(1)}, u32[]{:S(2)}, u32[]{:S(2)}) collective-permute-start(f32[2,1,128]{2,1,0:T(1,128)S(1)} %slice.204), channel_id=1, source_target_pairs={{0,16},{16,32},{32,48},{48,64},{64,80},{80,96},{96,112},{1,17},{17... | collective-permute-start | bytes 3080 | tf_op jit(solution)/shard_map/while/body/eval_jaxpr/ppermute | solution.py:15
  180.6 10.5 %collective-permute-start = (f32[2,1,128]{2,1,0:T(1,128)S(1)}, f32[2,1,128]{2,1,0:T(1,128)S(1)}, u32[]{:S(2)}, u32[]{:S(2)}) collective-permute-start(f32[2,1,128]{2,1,0:T(1,128)S(1)} %slice.201), channel_id=1, source_target_pairs={{16,0},{32,16},{48,32},{64,48},{80,64},{96,80},{112,96},{17,1},{33... | collective-permute-start | bytes 3080 | tf_op jit(solution)/shard_map/while/body/eval_jaxpr/ppermute | solution.py:15
  182.7 10.8 %collective-permute-start.1 = (f32[2,512]{1,0:T(2,128)S(1)}, f32[2,512]{1,0:T(2,128)S(1)}, u32[]{:S(2)}, u32[]{:S(2)}) collective-permute-start(f32[2,512]{1,0:T(2,128)S(1)} %slice_reduce_fusion.6), channel_id=1, source_target_pairs={{1,0},{2,1},{3,2},{4,3},{5,4},{6,5},{7,6},{8,7},{9,8},{10,9},{11,1... | collective-permute-start | bytes 12296 | tf_op jit(solution)/shard_map/while/body/eval_jaxpr/ppermute | solution.py:15
  191.3 7.3 %collective-permute-start.2 = (f32[2,512]{1,0:T(2,128)S(1)}, f32[2,512]{1,0:T(2,128)S(1)}, u32[]{:S(2)}, u32[]{:S(2)}) collective-permute-start(f32[2,512]{1,0:T(2,128)S(1)} %fusion.42), channel_id=1, source_target_pairs={{1,0},{2,1},{3,2},{4,3},{5,4},{6,5},{7,6},{8,7},{9,8},{10,9},{11,1... | collective-permute-start | bytes 12296 | tf_op jit(solution)/shard_map/while/body/eval_jaxpr/ppermute | solution.py:15
  211.7 6.5 %collective-permute-start.3 = (f32[2,512]{1,0:T(2,128)S(1)}, f32[2,512]{1,0:T(2,128)S(1)}, u32[]{:S(2)}, u32[]{:S(2)}) collective-permute-start(f32[2,512]{1,0:T(2,128)S(1)} %slice_reduce_fusion.7), channel_id=1, source_target_pairs={{0,1},{1,2},{2,3},{3,4},{4,5},{5,6},{6,7},{7,8},{8,9},{9,10},{10,1... | collective-permute-start | bytes 12296 | tf_op jit(solution)/shard_map/while/body/eval_jaxpr/ppermute | solution.py:15
  218.9 10.0 %collective-permute-start.4 = (f32[2,512]{1,0:T(2,128)S(1)}, f32[2,512]{1,0:T(2,128)S(1)}, u32[]{:S(2)}, u32[]{:S(2)}) collective-permute-start(f32[2,512]{1,0:T(2,128)S(1)} %slice_reduce_fusion.8), channel_id=1, source_target_pairs={{0,1},{1,2},{2,3},{3,4},{4,5},{5,6},{6,7},{7,8},{8,9},{9,10},{10,1... | collective-permute-start | bytes 12296 | tf_op jit(solution)/shard_map/while/body/eval_jaxpr/ppermute | solution.py:15
  225.5 6.4 %collective-permute-start.5 = (f32[2,1,128]{2,1,0:T(1,128)S(1)}, f32[2,1,128]{2,1,0:T(1,128)S(1)}, u32[]{:S(2)}, u32[]{:S(2)}) collective-permute-start(f32[2,1,128]{2,1,0:T(1,128)S(1)} %slice.204), channel_id=1, source_target_pairs={{0,16},{16,32},{32,48},{48,64},{64,80},{80,96},{96,112},{1,17},{17... | collective-permute-start | bytes 3080 | tf_op jit(solution)/shard_map/while/body/eval_jaxpr/ppermute | solution.py:15
  232.4 10.5 %collective-permute-start = (f32[2,1,128]{2,1,0:T(1,128)S(1)}, f32[2,1,128]{2,1,0:T(1,128)S(1)}, u32[]{:S(2)}, u32[]{:S(2)}) collective-permute-start(f32[2,1,128]{2,1,0:T(1,128)S(1)} %slice.201), channel_id=1, source_target_pairs={{16,0},{32,16},{48,32},{64,48},{80,64},{96,80},{112,96},{17,1},{33... | collective-permute-start | bytes 3080 | tf_op jit(solution)/shard_map/while/body/eval_jaxpr/ppermute | solution.py:15
  234.6 10.7 %collective-permute-start.1 = (f32[2,512]{1,0:T(2,128)S(1)}, f32[2,512]{1,0:T(2,128)S(1)}, u32[]{:S(2)}, u32[]{:S(2)}) collective-permute-start(f32[2,512]{1,0:T(2,128)S(1)} %slice_reduce_fusion.6), channel_id=1, source_target_pairs={{1,0},{2,1},{3,2},{4,3},{5,4},{6,5},{7,6},{8,7},{9,8},{10,9},{11,1... | collective-permute-start | bytes 12296 | tf_op jit(solution)/shard_map/while/body/eval_jaxpr/ppermute | solution.py:15
  243.1 7.3 %collective-permute-start.2 = (f32[2,512]{1,0:T(2,128)S(1)}, f32[2,512]{1,0:T(2,128)S(1)}, u32[]{:S(2)}, u32[]{:S(2)}) collective-permute-start(f32[2,512]{1,0:T(2,128)S(1)} %fusion.42), channel_id=1, source_target_pairs={{1,0},{2,1},{3,2},{4,3},{5,4},{6,5},{7,6},{8,7},{9,8},{10,9},{11,1... | collective-permute-start | bytes 12296 | tf_op jit(solution)/shard_map/while/body/eval_jaxpr/ppermute | solution.py:15
  263.5 6.5 %collective-permute-start.3 = (f32[2,512]{1,0:T(2,128)S(1)}, f32[2,512]{1,0:T(2,128)S(1)}, u32[]{:S(2)}, u32[]{:S(2)}) collective-permute-start(f32[2,512]{1,0:T(2,128)S(1)} %slice_reduce_fusion.7), channel_id=1, source_target_pairs={{0,1},{1,2},{2,3},{3,4},{4,5},{5,6},{6,7},{7,8},{8,9},{9,10},{10,1... | collective-permute-start | bytes 12296 | tf_op jit(solution)/shard_map/while/body/eval_jaxpr/ppermute | solution.py:15
  270.8 10.0 %collective-permute-start.4 = (f32[2,512]{1,0:T(2,128)S(1)}, f32[2,512]{1,0:T(2,128)S(1)}, u32[]{:S(2)}, u32[]{:S(2)}) collective-permute-start(f32[2,512]{1,0:T(2,128)S(1)} %slice_reduce_fusion.8), channel_id=1, source_target_pairs={{0,1},{1,2},{2,3},{3,4},{4,5},{5,6},{6,7},{7,8},{8,9},{9,10},{10,1... | collective-permute-start | bytes 12296 | tf_op jit(solution)/shard_map/while/body/eval_jaxpr/ppermute | solution.py:15
  277.4 6.4 %collective-permute-start.5 = (f32[2,1,128]{2,1,0:T(1,128)S(1)}, f32[2,1,128]{2,1,0:T(1,128)S(1)}, u32[]{:S(2)}, u32[]{:S(2)}) collective-permute-start(f32[2,1,128]{2,1,0:T(1,128)S(1)} %slice.204), channel_id=1, source_target_pairs={{0,16},{16,32},{32,48},{48,64},{64,80},{80,96},{96,112},{1,17},{17... | collective-permute-start | bytes 3080 | tf_op jit(solution)/shard_map/while/body/eval_jaxpr/ppermute | solution.py:15
  284.3 10.5 %collective-permute-start = (f32[2,1,128]{2,1,0:T(1,128)S(1)}, f32[2,1,128]{2,1,0:T(1,128)S(1)}, u32[]{:S(2)}, u32[]{:S(2)}) collective-permute-start(f32[2,1,128]{2,1,0:T(1,128)S(1)} %slice.201), channel_id=1, source_target_pairs={{16,0},{32,16},{48,32},{64,48},{80,64},{96,80},{112,96},{17,1},{33... | collective-permute-start | bytes 3080 | tf_op jit(solution)/shard_map/while/body/eval_jaxpr/ppermute | solution.py:15
  286.4 10.7 %collective-permute-start.1 = (f32[2,512]{1,0:T(2,128)S(1)}, f32[2,512]{1,0:T(2,128)S(1)}, u32[]{:S(2)}, u32[]{:S(2)}) collective-permute-start(f32[2,512]{1,0:T(2,128)S(1)} %slice_reduce_fusion.6), channel_id=1, source_target_pairs={{1,0},{2,1},{3,2},{4,3},{5,4},{6,5},{7,6},{8,7},{9,8},{10,9},{11,1... | collective-permute-start | bytes 12296 | tf_op jit(solution)/shard_map/while/body/eval_jaxpr/ppermute | solution.py:15
  295.0 7.3 %collective-permute-start.2 = (f32[2,512]{1,0:T(2,128)S(1)}, f32[2,512]{1,0:T(2,128)S(1)}, u32[]{:S(2)}, u32[]{:S(2)}) collective-permute-start(f32[2,512]{1,0:T(2,128)S(1)} %fusion.42), channel_id=1, source_target_pairs={{1,0},{2,1},{3,2},{4,3},{5,4},{6,5},{7,6},{8,7},{9,8},{10,9},{11,1... | collective-permute-start | bytes 12296 | tf_op jit(solution)/shard_map/while/body/eval_jaxpr/ppermute | solution.py:15
  315.4 6.5 %collective-permute-start.3 = (f32[2,512]{1,0:T(2,128)S(1)}, f32[2,512]{1,0:T(2,128)S(1)}, u32[]{:S(2)}, u32[]{:S(2)}) collective-permute-start(f32[2,512]{1,0:T(2,128)S(1)} %slice_reduce_fusion.7), channel_id=1, source_target_pairs={{0,1},{1,2},{2,3},{3,4},{4,5},{5,6},{6,7},{7,8},{8,9},{9,10},{10,1... | collective-permute-start | bytes 12296 | tf_op jit(solution)/shard_map/while/body/eval_jaxpr/ppermute | solution.py:15
  322.7 10.0 %collective-permute-start.4 = (f32[2,512]{1,0:T(2,128)S(1)}, f32[2,512]{1,0:T(2,128)S(1)}, u32[]{:S(2)}, u32[]{:S(2)}) collective-permute-start(f32[2,512]{1,0:T(2,128)S(1)} %slice_reduce_fusion.8), channel_id=1, source_target_pairs={{0,1},{1,2},{2,3},{3,4},{4,5},{5,6},{6,7},{7,8},{8,9},{9,10},{10,1... | collective-permute-start | bytes 12296 | tf_op jit(solution)/shard_map/while/body/eval_jaxpr/ppermute | solution.py:15
  329.3 6.4 %collective-permute-start.5 = (f32[2,1,128]{2,1,0:T(1,128)S(1)}, f32[2,1,128]{2,1,0:T(1,128)S(1)}, u32[]{:S(2)}, u32[]{:S(2)}) collective-permute-start(f32[2,1,128]{2,1,0:T(1,128)S(1)} %slice.204), channel_id=1, source_target_pairs={{0,16},{16,32},{32,48},{48,64},{64,80},{80,96},{96,112},{1,17},{17... | collective-permute-start | bytes 3080 | tf_op jit(solution)/shard_map/while/body/eval_jaxpr/ppermute | solution.py:15
  336.2 10.5 %collective-permute-start = (f32[2,1,128]{2,1,0:T(1,128)S(1)}, f32[2,1,128]{2,1,0:T(1,128)S(1)}, u32[]{:S(2)}, u32[]{:S(2)}) collective-permute-start(f32[2,1,128]{2,1,0:T(1,128)S(1)} %slice.201), channel_id=1, source_target_pairs={{16,0},{32,16},{48,32},{64,48},{80,64},{96,80},{112,96},{17,1},{33... | collective-permute-start | bytes 3080 | tf_op jit(solution)/shard_map/while/body/eval_jaxpr/ppermute | solution.py:15
  338.3 10.7 %collective-permute-start.1 = (f32[2,512]{1,0:T(2,128)S(1)}, f32[2,512]{1,0:T(2,128)S(1)}, u32[]{:S(2)}, u32[]{:S(2)}) collective-permute-start(f32[2,512]{1,0:T(2,128)S(1)} %slice_reduce_fusion.6), channel_id=1, source_target_pairs={{1,0},{2,1},{3,2},{4,3},{5,4},{6,5},{7,6},{8,7},{9,8},{10,9},{11,1... | collective-permute-start | bytes 12296 | tf_op jit(solution)/shard_map/while/body/eval_jaxpr/ppermute | solution.py:15
  346.9 7.3 %collective-permute-start.2 = (f32[2,512]{1,0:T(2,128)S(1)}, f32[2,512]{1,0:T(2,128)S(1)}, u32[]{:S(2)}, u32[]{:S(2)}) collective-permute-start(f32[2,512]{1,0:T(2,128)S(1)} %fusion.42), channel_id=1, source_target_pairs={{1,0},{2,1},{3,2},{4,3},{5,4},{6,5},{7,6},{8,7},{9,8},{10,9},{11,1... | collective-permute-start | bytes 12296 | tf_op jit(solution)/shard_map/while/body/eval_jaxpr/ppermute | solution.py:15
  367.2 6.5 %collective-permute-start.3 = (f32[2,512]{1,0:T(2,128)S(1)}, f32[2,512]{1,0:T(2,128)S(1)}, u32[]{:S(2)}, u32[]{:S(2)}) collective-permute-start(f32[2,512]{1,0:T(2,128)S(1)} %slice_reduce_fusion.7), channel_id=1, source_target_pairs={{0,1},{1,2},{2,3},{3,4},{4,5},{5,6},{6,7},{7,8},{8,9},{9,10},{10,1... | collective-permute-start | bytes 12296 | tf_op jit(solution)/shard_map/while/body/eval_jaxpr/ppermute | solution.py:15
  374.5 10.0 %collective-permute-start.4 = (f32[2,512]{1,0:T(2,128)S(1)}, f32[2,512]{1,0:T(2,128)S(1)}, u32[]{:S(2)}, u32[]{:S(2)}) collective-permute-start(f32[2,512]{1,0:T(2,128)S(1)} %slice_reduce_fusion.8), channel_id=1, source_target_pairs={{0,1},{1,2},{2,3},{3,4},{4,5},{5,6},{6,7},{7,8},{8,9},{9,10},{10,1... | collective-permute-start | bytes 12296 | tf_op jit(solution)/shard_map/while/body/eval_jaxpr/ppermute | solution.py:15
  381.1 6.4 %collective-permute-start.5 = (f32[2,1,128]{2,1,0:T(1,128)S(1)}, f32[2,1,128]{2,1,0:T(1,128)S(1)}, u32[]{:S(2)}, u32[]{:S(2)}) collective-permute-start(f32[2,1,128]{2,1,0:T(1,128)S(1)} %slice.204), channel_id=1, source_target_pairs={{0,16},{16,32},{32,48},{48,64},{64,80},{80,96},{96,112},{1,17},{17... | collective-permute-start | bytes 3080 | tf_op jit(solution)/shard_map/while/body/eval_jaxpr/ppermute | solution.py:15
  388.0 10.5 %collective-permute-start = (f32[2,1,128]{2,1,0:T(1,128)S(1)}, f32[2,1,128]{2,1,0:T(1,128)S(1)}, u32[]{:S(2)}, u32[]{:S(2)}) collective-permute-start(f32[2,1,128]{2,1,0:T(1,128)S(1)} %slice.201), channel_id=1, source_target_pairs={{16,0},{32,16},{48,32},{64,48},{80,64},{96,80},{112,96},{17,1},{33... | collective-permute-start | bytes 3080 | tf_op jit(solution)/shard_map/while/body/eval_jaxpr/ppermute | solution.py:15
  390.2 10.7 %collective-permute-start.1 = (f32[2,512]{1,0:T(2,128)S(1)}, f32[2,512]{1,0:T(2,128)S(1)}, u32[]{:S(2)}, u32[]{:S(2)}) collective-permute-start(f32[2,512]{1,0:T(2,128)S(1)} %slice_reduce_fusion.6), channel_id=1, source_target_pairs={{1,0},{2,1},{3,2},{4,3},{5,4},{6,5},{7,6},{8,7},{9,8},{10,9},{11,1... | collective-permute-start | bytes 12296 | tf_op jit(solution)/shard_map/while/body/eval_jaxpr/ppermute | solution.py:15
  398.7 7.3 %collective-permute-start.2 = (f32[2,512]{1,0:T(2,128)S(1)}, f32[2,512]{1,0:T(2,128)S(1)}, u32[]{:S(2)}, u32[]{:S(2)}) collective-permute-start(f32[2,512]{1,0:T(2,128)S(1)} %fusion.42), channel_id=1, source_target_pairs={{1,0},{2,1},{3,2},{4,3},{5,4},{6,5},{7,6},{8,7},{9,8},{10,9},{11,1... | collective-permute-start | bytes 12296 | tf_op jit(solution)/shard_map/while/body/eval_jaxpr/ppermute | solution.py:15
  419.1 6.5 %collective-permute-start.3 = (f32[2,512]{1,0:T(2,128)S(1)}, f32[2,512]{1,0:T(2,128)S(1)}, u32[]{:S(2)}, u32[]{:S(2)}) collective-permute-start(f32[2,512]{1,0:T(2,128)S(1)} %slice_reduce_fusion.7), channel_id=1, source_target_pairs={{0,1},{1,2},{2,3},{3,4},{4,5},{5,6},{6,7},{7,8},{8,9},{9,10},{10,1... | collective-permute-start | bytes 12296 | tf_op jit(solution)/shard_map/while/body/eval_jaxpr/ppermute | solution.py:15
  426.4 10.0 %collective-permute-start.4 = (f32[2,512]{1,0:T(2,128)S(1)}, f32[2,512]{1,0:T(2,128)S(1)}, u32[]{:S(2)}, u32[]{:S(2)}) collective-permute-start(f32[2,512]{1,0:T(2,128)S(1)} %slice_reduce_fusion.8), channel_id=1, source_target_pairs={{0,1},{1,2},{2,3},{3,4},{4,5},{5,6},{6,7},{7,8},{8,9},{9,10},{10,1... | collective-permute-start | bytes 12296 | tf_op jit(solution)/shard_map/while/body/eval_jaxpr/ppermute | solution.py:15
  433.0 6.4 %collective-permute-start.5 = (f32[2,1,128]{2,1,0:T(1,128)S(1)}, f32[2,1,128]{2,1,0:T(1,128)S(1)}, u32[]{:S(2)}, u32[]{:S(2)}) collective-permute-start(f32[2,1,128]{2,1,0:T(1,128)S(1)} %slice.204), channel_id=1, source_target_pairs={{0,16},{16,32},{32,48},{48,64},{64,80},{80,96},{96,112},{1,17},{17... | collective-permute-start | bytes 3080 | tf_op jit(solution)/shard_map/while/body/eval_jaxpr/ppermute | solution.py:15
  439.9 10.5 %collective-permute-start = (f32[2,1,128]{2,1,0:T(1,128)S(1)}, f32[2,1,128]{2,1,0:T(1,128)S(1)}, u32[]{:S(2)}, u32[]{:S(2)}) collective-permute-start(f32[2,1,128]{2,1,0:T(1,128)S(1)} %slice.201), channel_id=1, source_target_pairs={{16,0},{32,16},{48,32},{64,48},{80,64},{96,80},{112,96},{17,1},{33... | collective-permute-start | bytes 3080 | tf_op jit(solution)/shard_map/while/body/eval_jaxpr/ppermute | solution.py:15
  442.0 10.7 %collective-permute-start.1 = (f32[2,512]{1,0:T(2,128)S(1)}, f32[2,512]{1,0:T(2,128)S(1)}, u32[]{:S(2)}, u32[]{:S(2)}) collective-permute-start(f32[2,512]{1,0:T(2,128)S(1)} %slice_reduce_fusion.6), channel_id=1, source_target_pairs={{1,0},{2,1},{3,2},{4,3},{5,4},{6,5},{7,6},{8,7},{9,8},{10,9},{11,1... | collective-permute-start | bytes 12296 | tf_op jit(solution)/shard_map/while/body/eval_jaxpr/ppermute | solution.py:15
  450.6 7.3 %collective-permute-start.2 = (f32[2,512]{1,0:T(2,128)S(1)}, f32[2,512]{1,0:T(2,128)S(1)}, u32[]{:S(2)}, u32[]{:S(2)}) collective-permute-start(f32[2,512]{1,0:T(2,128)S(1)} %fusion.42), channel_id=1, source_target_pairs={{1,0},{2,1},{3,2},{4,3},{5,4},{6,5},{7,6},{8,7},{9,8},{10,9},{11,1... | collective-permute-start | bytes 12296 | tf_op jit(solution)/shard_map/while/body/eval_jaxpr/ppermute | solution.py:15
  471.0 6.5 %collective-permute-start.3 = (f32[2,512]{1,0:T(2,128)S(1)}, f32[2,512]{1,0:T(2,128)S(1)}, u32[]{:S(2)}, u32[]{:S(2)}) collective-permute-start(f32[2,512]{1,0:T(2,128)S(1)} %slice_reduce_fusion.7), channel_id=1, source_target_pairs={{0,1},{1,2},{2,3},{3,4},{4,5},{5,6},{6,7},{7,8},{8,9},{9,10},{10,1... | collective-permute-start | bytes 12296 | tf_op jit(solution)/shard_map/while/body/eval_jaxpr/ppermute | solution.py:15
  478.3 10.0 %collective-permute-start.4 = (f32[2,512]{1,0:T(2,128)S(1)}, f32[2,512]{1,0:T(2,128)S(1)}, u32[]{:S(2)}, u32[]{:S(2)}) collective-permute-start(f32[2,512]{1,0:T(2,128)S(1)} %slice_reduce_fusion.8), channel_id=1, source_target_pairs={{0,1},{1,2},{2,3},{3,4},{4,5},{5,6},{6,7},{7,8},{8,9},{9,10},{10,1... | collective-permute-start | bytes 12296 | tf_op jit(solution)/shard_map/while/body/eval_jaxpr/ppermute | solution.py:15
  484.9 6.4 %collective-permute-start.5 = (f32[2,1,128]{2,1,0:T(1,128)S(1)}, f32[2,1,128]{2,1,0:T(1,128)S(1)}, u32[]{:S(2)}, u32[]{:S(2)}) collective-permute-start(f32[2,1,128]{2,1,0:T(1,128)S(1)} %slice.204), channel_id=1, source_target_pairs={{0,16},{16,32},{32,48},{48,64},{64,80},{80,96},{96,112},{1,17},{17... | collective-permute-start | bytes 3080 | tf_op jit(solution)/shard_map/while/body/eval_jaxpr/ppermute | solution.py:15
  491.8 10.5 %collective-permute-start = (f32[2,1,128]{2,1,0:T(1,128)S(1)}, f32[2,1,128]{2,1,0:T(1,128)S(1)}, u32[]{:S(2)}, u32[]{:S(2)}) collective-permute-start(f32[2,1,128]{2,1,0:T(1,128)S(1)} %slice.201), channel_id=1, source_target_pairs={{16,0},{32,16},{48,32},{64,48},{80,64},{96,80},{112,96},{17,1},{33... | collective-permute-start | bytes 3080 | tf_op jit(solution)/shard_map/while/body/eval_jaxpr/ppermute | solution.py:15
  493.9 10.7 %collective-permute-start.1 = (f32[2,512]{1,0:T(2,128)S(1)}, f32[2,512]{1,0:T(2,128)S(1)}, u32[]{:S(2)}, u32[]{:S(2)}) collective-permute-start(f32[2,512]{1,0:T(2,128)S(1)} %slice_reduce_fusion.6), channel_id=1, source_target_pairs={{1,0},{2,1},{3,2},{4,3},{5,4},{6,5},{7,6},{8,7},{9,8},{10,9},{11,1... | collective-permute-start | bytes 12296 | tf_op jit(solution)/shard_map/while/body/eval_jaxpr/ppermute | solution.py:15
  502.5 7.3 %collective-permute-start.2 = (f32[2,512]{1,0:T(2,128)S(1)}, f32[2,512]{1,0:T(2,128)S(1)}, u32[]{:S(2)}, u32[]{:S(2)}) collective-permute-start(f32[2,512]{1,0:T(2,128)S(1)} %fusion.42), channel_id=1, source_target_pairs={{1,0},{2,1},{3,2},{4,3},{5,4},{6,5},{7,6},{8,7},{9,8},{10,9},{11,1... | collective-permute-start | bytes 12296 | tf_op jit(solution)/shard_map/while/body/eval_jaxpr/ppermute | solution.py:15
  522.8 6.5 %collective-permute-start.3 = (f32[2,512]{1,0:T(2,128)S(1)}, f32[2,512]{1,0:T(2,128)S(1)}, u32[]{:S(2)}, u32[]{:S(2)}) collective-permute-start(f32[2,512]{1,0:T(2,128)S(1)} %slice_reduce_fusion.7), channel_id=1, source_target_pairs={{0,1},{1,2},{2,3},{3,4},{4,5},{5,6},{6,7},{7,8},{8,9},{9,10},{10,1... | collective-permute-start | bytes 12296 | tf_op jit(solution)/shard_map/while/body/eval_jaxpr/ppermute | solution.py:15
  530.1 10.0 %collective-permute-start.4 = (f32[2,512]{1,0:T(2,128)S(1)}, f32[2,512]{1,0:T(2,128)S(1)}, u32[]{:S(2)}, u32[]{:S(2)}) collective-permute-start(f32[2,512]{1,0:T(2,128)S(1)} %slice_reduce_fusion.8), channel_id=1, source_target_pairs={{0,1},{1,2},{2,3},{3,4},{4,5},{5,6},{6,7},{7,8},{8,9},{9,10},{10,1... | collective-permute-start | bytes 12296 | tf_op jit(solution)/shard_map/while/body/eval_jaxpr/ppermute | solution.py:15
  536.7 6.4 %collective-permute-start.5 = (f32[2,1,128]{2,1,0:T(1,128)S(1)}, f32[2,1,128]{2,1,0:T(1,128)S(1)}, u32[]{:S(2)}, u32[]{:S(2)}) collective-permute-start(f32[2,1,128]{2,1,0:T(1,128)S(1)} %slice.204), channel_id=1, source_target_pairs={{0,16},{16,32},{32,48},{48,64},{64,80},{80,96},{96,112},{1,17},{17... | collective-permute-start | bytes 3080 | tf_op jit(solution)/shard_map/while/body/eval_jaxpr/ppermute | solution.py:15
  543.6 10.5 %collective-permute-start = (f32[2,1,128]{2,1,0:T(1,128)S(1)}, f32[2,1,128]{2,1,0:T(1,128)S(1)}, u32[]{:S(2)}, u32[]{:S(2)}) collective-permute-start(f32[2,1,128]{2,1,0:T(1,128)S(1)} %slice.201), channel_id=1, source_target_pairs={{16,0},{32,16},{48,32},{64,48},{80,64},{96,80},{112,96},{17,1},{33... | collective-permute-start | bytes 3080 | tf_op jit(solution)/shard_map/while/body/eval_jaxpr/ppermute | solution.py:15
  545.8 10.7 %collective-permute-start.1 = (f32[2,512]{1,0:T(2,128)S(1)}, f32[2,512]{1,0:T(2,128)S(1)}, u32[]{:S(2)}, u32[]{:S(2)}) collective-permute-start(f32[2,512]{1,0:T(2,128)S(1)} %slice_reduce_fusion.6), channel_id=1, source_target_pairs={{1,0},{2,1},{3,2},{4,3},{5,4},{6,5},{7,6},{8,7},{9,8},{10,9},{11,1... | collective-permute-start | bytes 12296 | tf_op jit(solution)/shard_map/while/body/eval_jaxpr/ppermute | solution.py:15
  554.3 7.3 %collective-permute-start.2 = (f32[2,512]{1,0:T(2,128)S(1)}, f32[2,512]{1,0:T(2,128)S(1)}, u32[]{:S(2)}, u32[]{:S(2)}) collective-permute-start(f32[2,512]{1,0:T(2,128)S(1)} %fusion.42), channel_id=1, source_target_pairs={{1,0},{2,1},{3,2},{4,3},{5,4},{6,5},{7,6},{8,7},{9,8},{10,9},{11,1... | collective-permute-start | bytes 12296 | tf_op jit(solution)/shard_map/while/body/eval_jaxpr/ppermute | solution.py:15
  574.7 6.5 %collective-permute-start.3 = (f32[2,512]{1,0:T(2,128)S(1)}, f32[2,512]{1,0:T(2,128)S(1)}, u32[]{:S(2)}, u32[]{:S(2)}) collective-permute-start(f32[2,512]{1,0:T(2,128)S(1)} %slice_reduce_fusion.7), channel_id=1, source_target_pairs={{0,1},{1,2},{2,3},{3,4},{4,5},{5,6},{6,7},{7,8},{8,9},{9,10},{10,1... | collective-permute-start | bytes 12296 | tf_op jit(solution)/shard_map/while/body/eval_jaxpr/ppermute | solution.py:15
  582.0 10.0 %collective-permute-start.4 = (f32[2,512]{1,0:T(2,128)S(1)}, f32[2,512]{1,0:T(2,128)S(1)}, u32[]{:S(2)}, u32[]{:S(2)}) collective-permute-start(f32[2,512]{1,0:T(2,128)S(1)} %slice_reduce_fusion.8), channel_id=1, source_target_pairs={{0,1},{1,2},{2,3},{3,4},{4,5},{5,6},{6,7},{7,8},{8,9},{9,10},{10,1... | collective-permute-start | bytes 12296 | tf_op jit(solution)/shard_map/while/body/eval_jaxpr/ppermute | solution.py:15
  588.6 6.4 %collective-permute-start.5 = (f32[2,1,128]{2,1,0:T(1,128)S(1)}, f32[2,1,128]{2,1,0:T(1,128)S(1)}, u32[]{:S(2)}, u32[]{:S(2)}) collective-permute-start(f32[2,1,128]{2,1,0:T(1,128)S(1)} %slice.204), channel_id=1, source_target_pairs={{0,16},{16,32},{32,48},{48,64},{64,80},{80,96},{96,112},{1,17},{17... | collective-permute-start | bytes 3080 | tf_op jit(solution)/shard_map/while/body/eval_jaxpr/ppermute | solution.py:15
  (2 other events, 4.5 us)
